TPU v7x, 32 devices: a whole 2x2x4 slice. The times are simulated.
32 devices in a mesh: dp: 2 (over y), expert: 4 (over x, core), tensor: 4 (over z).
Axes of the slice: x: 2, y: 2, z: 4, core: 2. Of those that a mesh axis runs over, the one named last changes fastest.
Arguments:
- hidden_states: bfloat16 [256, 4096], P(('dp', 'expert'), 'tensor'), may hold values from -6 to 6
- chosen_experts: int32 [256, 2], P(('dp', 'expert')), may hold values from 0 to 3, all different within a row; in each aligned block of 32 rows (0 to 31, 32 to 63, ...) at most 16 rows name the same one
- choice_weights: float32 [256, 2], P(('dp', 'expert')), may hold values from 0.2 to 1
- gate_proj: bfloat16 [4, 4096, 8192], P('expert', None, ('dp', 'tensor')), may hold values from -0.09375 to 0.09375
- up_proj: bfloat16 [4, 4096, 8192], P('expert', None, ('dp', 'tensor')), may hold values from -0.09375 to 0.09375
- down_proj: bfloat16 [4, 8192, 4096], P('expert', 'dp', 'tensor'), may hold values from -0.0625 to 0.0625
Outputs:
- moe_output: bfloat16 [256, 4096], P(('dp', 'expert'), 'tensor')
Inputs may be any that keep to these rules, and one draw needn't show every extreme that they name: `chosen_experts`: each row names 2 different experts; among the 32 rows of one device no expert is named more than 16 times, a bound that some block reaches.
All inputs are finite; a program needn't handle non-finite values.
Results may differ from a plain program's by a relative error of at most 0.0058.
Values may be sent and summed in bfloat16 or wider, within the bound.
A program may use at most 64 MiB of HBM per device.

v0:
```python
import jax
import jax.numpy as jnp
from jax import lax
from jax.sharding import PartitionSpec as P

CAP = 16


def slot_tables(chosen_experts, experts, capacity):
    flat_ids = chosen_experts.reshape(-1)
    onehot = (flat_ids[:, None] == jnp.arange(experts, dtype=jnp.int32)[None, :]).astype(jnp.int32)
    before = jnp.cumsum(onehot, axis=0) - onehot
    position = jnp.sum(before * onehot, axis=1)
    return (flat_ids * capacity + position).reshape(chosen_experts.shape)


def body(hidden_states, chosen_experts, choice_weights, gate_proj, up_proj, down_proj):
    experts = lax.axis_size("expert")
    token_count = hidden_states.shape[0]
    feat_width = hidden_states.shape[1]
    slot_count = experts * CAP
    target = slot_tables(chosen_experts, experts, CAP)
    slot_ids = jnp.arange(slot_count, dtype=jnp.int32)
    placing = jnp.zeros((slot_count, token_count), jnp.float32)
    weights_table = jnp.zeros((token_count, slot_count), jnp.float32)
    for column in range(target.shape[1]):
        placing = placing + (slot_ids[:, None] == target[None, :, column]).astype(jnp.float32)
        weights_table = weights_table + jnp.where(
            target[:, column][:, None] == slot_ids[None, :],
            choice_weights[:, column][:, None],
            jnp.float32(0.0),
        )
    packed = jnp.dot(
        placing.astype(jnp.bfloat16), hidden_states, preferred_element_type=jnp.float32
    )
    packed = packed.astype(jnp.bfloat16).reshape(experts, CAP, feat_width)
    arrived = lax.all_to_all(packed, "expert", split_axis=0, concat_axis=0, tiled=True).reshape(
        slot_count, feat_width
    )
    gate_weights = gate_proj[0]
    up_weights = up_proj[0]
    down_weights = down_proj[0]
    features = lax.all_gather(arrived, "tensor", axis=1, tiled=True)
    shards = lax.all_gather(features, "dp", axis=0, tiled=True)
    gate_part = jnp.dot(shards, gate_weights, preferred_element_type=jnp.float32)
    up_part = jnp.dot(shards, up_weights, preferred_element_type=jnp.float32)
    activated = (jax.nn.silu(gate_part) * up_part).astype(jnp.bfloat16)
    unit_rows = lax.all_gather(activated, "tensor", axis=1, tiled=True)
    summed = lax.psum_scatter(
        jnp.dot(unit_rows, down_weights, preferred_element_type=jnp.float32),
        "dp",
        scatter_dimension=0,
        tiled=True,
    )
    outgoing = summed.astype(jnp.bfloat16).reshape(experts, CAP, feat_width)
    returned = lax.all_to_all(outgoing, "expert", split_axis=0, concat_axis=0, tiled=True).reshape(
        slot_count, feat_width
    )
    combined = jnp.dot(
        weights_table,
        returned.astype(jnp.float32),
        precision=lax.Precision.HIGHEST,
        preferred_element_type=jnp.float32,
    )
    return combined.astype(jnp.bfloat16)


def solution(mesh):
    in_specs = (
        P(("dp", "expert"), "tensor"),
        P(("dp", "expert"), None),
        P(("dp", "expert"), None),
        P("expert", None, ("dp", "tensor")),
        P("expert", None, ("dp", "tensor")),
        P("expert", "dp", "tensor"),
    )
    out_specs = P(("dp", "expert"), "tensor")
    return jax.shard_map(body, mesh=mesh, in_specs=in_specs, out_specs=out_specs, check_vma=False)
```

profile of v0, /device:TPU:0, one launch (start us, length us, event | category | flops | bytes accessed | tf_op | source)
XLA Modules:
  0.0 131.8 jit_solution(14651087666373031079)
XLA Ops:
  6.5 0.8 copy.13
  7.3 0.1 eq.71
  7.4 0.1 fusion.12
  7.5 0.1 reduce_window_sum.11
  7.6 0.2 select_reduce_fusion
  7.8 0.1 reduce_sum.12
  7.9 0.1 copy.14
  8.0 0.7 multiply_add_fusion
  8.7 0.2 convolution_convert_fusion
  8.9 8.6 %all_to_all.10 = bf16[4,16,1024]{2,1,0:T(8,128)(2,1)S(1)} all-to-all(bf16[4,16,1024]{2,1,0:T(8,128)(2,1)S(1)} %bitcast.31), channel_id=1, replica_groups=mesh['dp'=2,'expert'=4,'tensor'=4] {'expert'}, dimensions={0} | all-to-all | bytes 262144 | tf_op jit(solution)/shard_map/all_to_all | solution.py:37
  17.5 16.2 %all_gather.9 = bf16[64,4096]{1,0:T(8,128)(2,1)} all-gather(bf16[64,1024]{1,0:T(8,128)(2,1)S(1)} %bitcast.30), channel_id=1, replica_groups=mesh['dp'=2,'expert'=4,'tensor'=4] {'tensor'}, dimensions={1}, use_global_device_ids=true | all-gather | bytes 655360 | tf_op jit(solution)/shard_map/all_gather | solution.py:43
  33.8 0.0 all-gather.3.cloned.1.call-update
  33.8 0.0 all-gather.5.cloned.1.call-start
  33.8 22.4 %all-gather.3.cloned.1.call-done = bf16[128,4096]{1,0:T(8,128)(2,1)} async-done(((bf16[64,4096]{1,0:T(8,128)(2,1)}), bf16[128,4096]{1,0:T(8,128)(2,1)}) %all-gather.3.cloned.1.call-update) | async-done | bytes 1048592 | tf_op jit(solution)/shard_map/all_gather | solution.py:44
  56.2 5.0 %fusion.4 = f32[128,1024]{1,0:T(8,128)S(1)} fusion(bf16[128,4096]{1,0:T(8,128)(2,1)} %all-gather.3.cloned.1.call-done, bf16[1,4096,1024]{2,1,0:T(8,128)(2,1)} %param.9), kind=kOutput, calls=%fused_computation.4 | convolution fusion | flops 1073741824 | bytes 9961472 | tf_op jit(solution)/shard_map/dot_general | solution.py:45
  61.2 5.5 %fusion.9 = bf16[128,1024]{1,0:T(8,128)(2,1)} fusion(bf16[128,4096]{1,0:T(8,128)(2,1)S(1)} %copy-done.1, bf16[1,4096,1024]{2,1,0:T(8,128)(2,1)} %param.10, f32[128,1024]{1,0:T(8,128)S(1)} %fusion.4), kind=kOutput, calls=%fused_computation.7 | convolution fusion | flops 1074528256 | bytes 10223616 | tf_op jit(solution)/shard_map/dot_general | solution.py:46
  66.8 0.0 reduce-scatter.2.cloned.1.call-start
  66.8 28.0 %all-gather.5.cloned.1.call-done = bf16[128,4096]{1,0:T(8,128)(2,1)} async-done(((bf16[128,1024]{1,0:T(8,128)(2,1)}), bf16[128,4096]{1,0:T(8,128)(2,1)}) %all-gather.5.cloned.1.call-update) | async-done | bytes 1048592 | tf_op jit(solution)/shard_map/all_gather | solution.py:48
  94.8 5.8 %fusion = f32[128,1024]{1,0:T(8,128)} fusion(bf16[128,4096]{1,0:T(8,128)(2,1)} %all-gather.5.cloned.1.call-done, bf16[1,4096,1024]{2,1,0:T(8,128)(2,1)} %param.11), kind=kOutput, calls=%fused_computation | convolution fusion | flops 1073741824 | bytes 9961472 | tf_op jit(solution)/shard_map/dot_general | solution.py:50
  100.7 14.2 %reduce-scatter.2.cloned.1.call-done = f32[64,1024]{1,0:T(8,128)} async-done(((f32[128,1024]{1,0:T(8,128)}), f32[64,1024]{1,0:T(8,128)}) %reduce-scatter.2.cloned.1.call-update) | async-done | bytes 262160 | tf_op jit(solution)/shard_map/reduce_scatter | solution.py:49
  114.9 1.6 %convert_element_type.31 = bf16[64,1024]{1,0:T(8,128)(2,1)} convert(f32[64,1024]{1,0:T(8,128)} %reduce-scatter.2.cloned.1.call-done) | non-fusion elementwise | flops 65536 | bytes 393216 | tf_op jit(solution)/shard_map/convert_element_type | solution.py:55
  116.5 3.3 %all-to-all-start.1 = ((bf16[4,16,1024]{2,1,0:T(8,128)(2,1)}), bf16[4,16,1024]{2,1,0:T(8,128)(2,1)S(1)}, u32[]{:S(2)}, u32[]{:S(2)}) async-start(bf16[4,16,1024]{2,1,0:T(8,128)(2,1)} %bitcast.9), calls=%async_computation.2 | async-start | bytes 262144 | tf_op jit(solution)/shard_map/all_to_all | solution.py:56
  119.8 4.6 %all-to-all-done.1 = bf16[4,16,1024]{2,1,0:T(8,128)(2,1)S(1)} async-done(((bf16[4,16,1024]{2,1,0:T(8,128)(2,1)}), bf16[4,16,1024]{2,1,0:T(8,128)(2,1)S(1)}, u32[]{:S(2)}, u32[]{:S(2)}) %all-to-all-start.1) | async-done | bytes 131104 | tf_op jit(solution)/shard_map/all_to_all | solution.py:56
  124.4 0.9 convolution_convert_fusion.1
  (11 shorter events, 0.1 us)
Async XLA Ops:
  6.5 2.2 %copy-start = (bf16[32,1024]{1,0:T(8,128)(2,1)S(1)}, bf16[32,1024]{1,0:T(8,128)(2,1)}, u32[]{:S(2)}) copy-start(bf16[32,1024]{1,0:T(8,128)(2,1)} %param.6) | copy-start | bytes 196612
  6.5 49.7 %all-gather.3.cloned.1.call-start = ((), (), s32[]{:S(2)}) async-start(), calls=%async_computation.3 | async-start | bytes 1572864 | tf_op jit(solution)/shard_map/all_gather | solution.py:44
  33.8 61.1 %all-gather.5.cloned.1.call-start = ((), (), s32[]{:S(2)}) async-start(), calls=%async_computation.4 | async-start | bytes 1310720 | tf_op jit(solution)/shard_map/all_gather | solution.py:48
  56.2 5.0 %copy-start.1 = (bf16[128,4096]{1,0:T(8,128)(2,1)S(1)}, bf16[128,4096]{1,0:T(8,128)(2,1)}, u32[]{:S(2)}) copy-start(bf16[128,4096]{1,0:T(8,128)(2,1)} %all-gather.3.cloned.1.call-done) | copy-start | bytes 3145732
  66.8 53.1 %copy-start.2 = (f32[32,2]{0,1:T(2,128)S(1)}, f32[32,2]{0,1:T(2,128)}, u32[]{:S(2)}) copy-start(f32[32,2]{0,1:T(2,128)} %param.8) | copy-start | bytes 772
  66.8 48.1 %reduce-scatter.2.cloned.1.call-start = ((), (), s32[]{:S(2)}) async-start(), calls=%async_computation.5 | async-start | bytes 786432 | tf_op jit(solution)/shard_map/reduce_scatter | solution.py:49
  116.5 7.9 %all-to-all-start.1 = ((bf16[4,16,1024]{2,1,0:T(8,128)(2,1)}), bf16[4,16,1024]{2,1,0:T(8,128)(2,1)S(1)}, u32[]{:S(2)}, u32[]{:S(2)}) async-start(bf16[4,16,1024]{2,1,0:T(8,128)(2,1)} %bitcast.9), calls=%async_computation.2 | async-start | bytes 262144 | tf_op jit(solution)/shard_map/all_to_all | solution.py:56
Sparse Core Ops, SparseCore 0:
  33.9 22.2 all-gather.2
  66.9 27.9 all-gather.4
  100.8 14.0 reduce-scatter.1
where the time goes:
time: 132 us
  waiting for transfers between devices  69.2 us (52%)
  blocking collectives  24.9 us (19%)
  matrix products  17.4 us (13%)
  between operations  13.2 us (10%)
  starting transfers between devices  3.41 us (3%)
  other arithmetic  2.66 us (2%)
    all_gather x1, waiting for transfers between devices, body(): unit_rows = lax.all_gather(activated, 'tensor', axis=1, tiled=True)  28 us
    all_gather x1, waiting for transfers between devices, body(): shards = lax.all_gather(features, 'dp', axis=0, tiled=True)  22.4 us
    all_gather x1, blocking collectives, body(): features = lax.all_gather(arrived, 'tensor', axis=1, tiled=True)  16.2 us
    reduce_scatter x1, waiting for transfers between devices, body(): lax.psum_scatter(jnp.dot(unit_rows, down_weights, preferred_element_type=...  14.2 us
    all_to_all x1, blocking collectives, body(): lax.all_to_all(packed, 'expert', split_axis=0, concat_axis=0, tiled=True)  8.64 us
    dot_general x1, matrix products, body(): jnp.dot(unit_rows, down_weights, preferred_element_type=jnp.float32)  5.79 us
    dot_general x1, matrix products, body(): up_part = jnp.dot(shards, up_weights, preferred_element_type=jnp.float32)  5.48 us
    dot_general x1, matrix products, body(): jnp.dot(shards, gate_weights, preferred_element_type=jnp.float32)  5.03 us
  transfers between devices with their start and end apart: 4, of which 4 were waited for; matrix products, arithmetic and copies ran while one was open for 0% of the time, Pallas kernels for 0%

commit v1 on v0

--- a/solution.py
+++ b/solution.py
@@ -41,7 +41,14 @@
     up_weights = up_proj[0]
     down_weights = down_proj[0]
     features = lax.all_gather(arrived, "tensor", axis=1, tiled=True)
-    shards = lax.all_gather(features, "dp", axis=0, tiled=True)
+    ways, here = (lax.axis_size("dp"), lax.axis_index("dp"))
+    shards, reach = (features, 1)
+    while reach < ways:
+        theirs = lax.ppermute(shards, "dp", [(d, d ^ reach) for d in range(ways)])
+        mine_first = jnp.concatenate([shards, theirs], axis=0)
+        theirs_first = jnp.concatenate([theirs, shards], axis=0)
+        shards = jnp.where(here & reach == 0, mine_first, theirs_first)
+        reach = 2 * reach
     gate_part = jnp.dot(shards, gate_weights, preferred_element_type=jnp.float32)
     up_part = jnp.dot(shards, up_weights, preferred_element_type=jnp.float32)
     activated = (jax.nn.silu(gate_part) * up_part).astype(jnp.bfloat16)

time: 132 us -> 120 us (0.909)
  waiting for transfers between devices: 69.2 us -> 56.4 us
  starting transfers between devices: 3.41 us -> 4.89 us
    all_gather x1 -> x0, waiting for transfers between devices: 22.4 us -> none  [body(): shards = lax.all_gather(features, 'dp', axis=0, tiled=True)]
    ppermute x0 -> x1, waiting for transfers between devices: none -> 9.77 us  [body(): theirs = lax.ppermute(shards, 'dp', [(d, d ^ reach) for d in range(ways)])]
    ppermute x0 -> x1, starting transfers between devices: none -> 1.52 us  [body(): theirs = lax.ppermute(shards, 'dp', [(d, d ^ reach) for d in range(ways)])]
where the time goes in v1:
time: 120 us
  waiting for transfers between devices  56.4 us (47%)
  blocking collectives  24.3 us (20%)
  matrix products  17 us (14%)
  between operations  13.5 us (11%)
  starting transfers between devices  4.89 us (4%)
  other arithmetic  2.66 us (2%)
    all_gather x1, waiting for transfers between devices, body(): unit_rows = lax.all_gather(activated, 'tensor', axis=1, tiled=True)  27.8 us
    all_gather x1, blocking collectives, body(): features = lax.all_gather(arrived, 'tensor', axis=1, tiled=True)  15.6 us
    reduce_scatter x1, waiting for transfers between devices, body(): lax.psum_scatter(jnp.dot(unit_rows, down_weights, preferred_element_type=...  14.2 us
    ppermute x1, waiting for transfers between devices, body(): theirs = lax.ppermute(shards, 'dp', [(d, d ^ reach) for d in range(ways)])  9.77 us
    all_to_all x1, blocking collectives, body(): lax.all_to_all(packed, 'expert', split_axis=0, concat_axis=0, tiled=True)  8.64 us
    dot_general x1, matrix products, body(): jnp.dot(unit_rows, down_weights, preferred_element_type=jnp.float32)  5.79 us
    dot_general x1, matrix products, body(): up_part = jnp.dot(shards, up_weights, preferred_element_type=jnp.float32)  5.45 us
    dot_general x1, matrix products, body(): jnp.dot(shards, gate_weights, preferred_element_type=jnp.float32)  4.68 us
  transfers between devices with their start and end apart: 4, of which 4 were waited for; matrix products, arithmetic and copies ran while one was open for 0% of the time, Pallas kernels for 0%

profile of v1, /device:TPU:0, one launch (start us, length us, event | category | flops | bytes accessed | tf_op | source)
XLA Modules:
  0.0 119.8 jit_solution(16973471661101983111)
XLA Ops:
  6.5 0.8 copy.13
  7.3 0.1 eq.74
  7.4 0.1 fusion.8
  7.5 0.1 reduce_window_sum.11
  7.6 0.2 select_reduce_fusion
  7.8 0.1 reduce_sum.12
  7.9 0.1 copy.14
  8.0 0.7 multiply_add_fusion
  8.7 0.2 convolution_convert_fusion
  8.9 8.6 %all_to_all.10 = bf16[4,16,1024]{2,1,0:T(8,128)(2,1)S(1)} all-to-all(bf16[4,16,1024]{2,1,0:T(8,128)(2,1)S(1)} %bitcast.27), channel_id=1, replica_groups=mesh['dp'=2,'expert'=4,'tensor'=4] {'expert'}, dimensions={0} | all-to-all | bytes 262144 | tf_op jit(solution)/shard_map/all_to_all | solution.py:37
  17.5 15.6 %all_gather.6 = bf16[64,4096]{1,0:T(8,128)(2,1)S(1)} all-gather(bf16[64,1024]{1,0:T(8,128)(2,1)S(1)} %bitcast.26), channel_id=1, replica_groups=mesh['dp'=2,'expert'=4,'tensor'=4] {'tensor'}, dimensions={1}, use_global_device_ids=true | all-gather | bytes 655360 | tf_op jit(solution)/shard_map/all_gather | solution.py:43
  33.1 1.5 %collective-permute-start = (bf16[64,4096]{1,0:T(8,128)(2,1)S(1)}, bf16[64,4096]{1,0:T(8,128)(2,1)S(1)}, u32[]{:S(2)}, u32[]{:S(2)}) collective-permute-start(bf16[64,4096]{1,0:T(8,128)(2,1)S(1)} %all_gather.6), channel_id=1, source_target_pairs={{0,16},{16,0},{1,17},{17,1},{2,18},{18,2},{3,19},{19,3},{4,20},{20... | collective-permute-start | bytes 1572872 | tf_op jit(solution)/shard_map/ppermute | solution.py:47
  34.7 9.8 %collective-permute-done = bf16[64,4096]{1,0:T(8,128)(2,1)S(1)} collective-permute-done((bf16[64,4096]{1,0:T(8,128)(2,1)S(1)}, bf16[64,4096]{1,0:T(8,128)(2,1)S(1)}, u32[]{:S(2)}, u32[]{:S(2)}) %collective-permute-start) | collective-permute-done | bytes 524320 | tf_op jit(solution)/shard_map/ppermute | solution.py:47
  44.4 4.7 %fusion.4 = f32[128,1024]{1,0:T(8,128)S(1)} fusion(bf16[1,4096,1024]{2,1,0:T(8,128)(2,1)} %param.9, bf16[64,4096]{1,0:T(8,128)(2,1)S(1)} %collective-permute-done, bf16[64,4096]{1,0:T(8,128)(2,1)S(1)} %all_gather.6, pred[]{:T(512)S(6)} %eq.86), kind=kOutput, calls=%fused_computation.4 | convolution fusion | flops 1078460416 | bytes 9961473 | tf_op jit(solution)/shard_map/dot_general | solution.py:52
  49.1 5.5 %multiply_convert_fusion = bf16[128,1024]{1,0:T(8,128)(2,1)} fusion(f32[128,1024]{1,0:T(8,128)S(1)} %fusion.4, bf16[1,4096,1024]{2,1,0:T(8,128)(2,1)} %param.10, bf16[64,4096]{1,0:T(8,128)(2,1)S(1)} %collective-permute-done, bf16[64,4096]{1,0:T(8,128)(2,1)S(1)} %all_gather.6, pred[]{:T(512)S(6)} %eq.86), kind=kOutput, calls=%fused_computation.9 | convolution fusion | flops 1079246848 | bytes 10223617 | tf_op jit(solution)/shard_map/dot_general | solution.py:53
  54.6 0.0 all-gather.2.cloned.1.call-update
  54.6 0.0 reduce-scatter.2.cloned.1.call-start
  54.7 27.8 %all-gather.2.cloned.1.call-done = bf16[128,4096]{1,0:T(8,128)(2,1)} async-done(((bf16[128,1024]{1,0:T(8,128)(2,1)}), bf16[128,4096]{1,0:T(8,128)(2,1)}) %all-gather.2.cloned.1.call-update) | async-done | bytes 1048592 | tf_op jit(solution)/shard_map/all_gather | solution.py:55
  82.5 5.8 %fusion = f32[128,1024]{1,0:T(8,128)} fusion(bf16[128,4096]{1,0:T(8,128)(2,1)} %all-gather.2.cloned.1.call-done, bf16[1,4096,1024]{2,1,0:T(8,128)(2,1)} %param.11), kind=kOutput, calls=%fused_computation | convolution fusion | flops 1073741824 | bytes 9961472 | tf_op jit(solution)/shard_map/dot_general | solution.py:57
  88.3 14.2 %reduce-scatter.2.cloned.1.call-done = f32[64,1024]{1,0:T(8,128)} async-done(((f32[128,1024]{1,0:T(8,128)}), f32[64,1024]{1,0:T(8,128)}) %reduce-scatter.2.cloned.1.call-update) | async-done | bytes 262160 | tf_op jit(solution)/shard_map/reduce_scatter | solution.py:56
  102.5 1.6 %convert_element_type.31 = bf16[64,1024]{1,0:T(8,128)(2,1)} convert(f32[64,1024]{1,0:T(8,128)} %reduce-scatter.2.cloned.1.call-done) | non-fusion elementwise | flops 65536 | bytes 393216 | tf_op jit(solution)/shard_map/convert_element_type | solution.py:62
  104.1 3.3 %all-to-all-start.1 = ((bf16[4,16,1024]{2,1,0:T(8,128)(2,1)}), bf16[4,16,1024]{2,1,0:T(8,128)(2,1)S(1)}, u32[]{:S(2)}, u32[]{:S(2)}) async-start(bf16[4,16,1024]{2,1,0:T(8,128)(2,1)} %bitcast.9), calls=%async_computation.2 | async-start | bytes 262144 | tf_op jit(solution)/shard_map/all_to_all | solution.py:63
  107.5 4.6 %all-to-all-done.1 = bf16[4,16,1024]{2,1,0:T(8,128)(2,1)S(1)} async-done(((bf16[4,16,1024]{2,1,0:T(8,128)(2,1)}), bf16[4,16,1024]{2,1,0:T(8,128)(2,1)S(1)}, u32[]{:S(2)}, u32[]{:S(2)}) %all-to-all-start.1) | async-done | bytes 131104 | tf_op jit(solution)/shard_map/all_to_all | solution.py:63
  112.0 0.9 convolution_convert_fusion.1
  (8 shorter events, 0.0 us)
Async XLA Ops:
  6.5 2.2 %copy-start = (bf16[32,1024]{1,0:T(8,128)(2,1)S(1)}, bf16[32,1024]{1,0:T(8,128)(2,1)}, u32[]{:S(2)}) copy-start(bf16[32,1024]{1,0:T(8,128)(2,1)} %param.6) | copy-start | bytes 196612
  6.5 75.9 %all-gather.2.cloned.1.call-start = ((), (), s32[]{:S(2)}) async-start(), calls=%async_computation.3 | async-start | bytes 1310720 | tf_op jit(solution)/shard_map/all_gather | solution.py:55
  33.1 11.3 %collective-permute-start = (bf16[64,4096]{1,0:T(8,128)(2,1)S(1)}, bf16[64,4096]{1,0:T(8,128)(2,1)S(1)}, u32[]{:S(2)}, u32[]{:S(2)}) collective-permute-start(bf16[64,4096]{1,0:T(8,128)(2,1)S(1)} %all_gather.6), channel_id=1, source_target_pairs={{0,16},{16,0},{1,17},{17,1},{2,18},{18,2},{3,19},{19,3},{4,20},{20... | collective-permute-start | bytes 1572872 | tf_op jit(solution)/shard_map/ppermute | solution.py:47
  54.6 52.8 %copy-start.1 = (f32[32,2]{0,1:T(2,128)S(1)}, f32[32,2]{0,1:T(2,128)}, u32[]{:S(2)}) copy-start(f32[32,2]{0,1:T(2,128)} %param.8) | copy-start | bytes 772
  54.6 47.9 %reduce-scatter.2.cloned.1.call-start = ((), (), s32[]{:S(2)}) async-start(), calls=%async_computation.4 | async-start | bytes 786432 | tf_op jit(solution)/shard_map/reduce_scatter | solution.py:56
  104.1 7.9 %all-to-all-start.1 = ((bf16[4,16,1024]{2,1,0:T(8,128)(2,1)}), bf16[4,16,1024]{2,1,0:T(8,128)(2,1)S(1)}, u32[]{:S(2)}, u32[]{:S(2)}) async-start(bf16[4,16,1024]{2,1,0:T(8,128)(2,1)} %bitcast.9), calls=%async_computation.2 | async-start | bytes 262144 | tf_op jit(solution)/shard_map/all_to_all | solution.py:63
Sparse Core Ops, SparseCore 0:
  54.7 27.7 all-gather.1
  88.4 14.0 reduce-scatter.1
